TPU v7x, 256 devices: a whole 4x4x8 slice. The times are simulated.
256 devices in a mesh: tile: 64 (over z, x, core), mem: 4 (over y).
Axes of the slice: x: 4, y: 4, z: 8, core: 2. Of those that a mesh axis runs over, the one named last changes fastest.
Arguments:
- footprints: bfloat16 [8192, 128, 128], P('tile'), may hold values from -0.1875 to 0.1875
- tile_row: int32 [8192], P('tile'), may hold values from 0 to 1023, as said below
- tile_col: int32 [8192], P('tile'), may hold values from 0 to 511, as said below
- prior_flux: bfloat16 [256, 65536], P('mem', 'tile'), may hold values from -12 to 12
- observed: float32 [256, 131072], P('mem', 'tile'), may hold values from -6 to 6
- precision_weight: int32 [131072], P('tile'), may hold values from 1 to 16
Outputs:
- gradient: float32 [256, 65536], P('mem', 'tile')
Inputs may be any that keep to these rules, and one draw needn't show every extreme that they name: Among the 128 tiles of each index of tile, at most 3 have a row block of one owner (owner = tile_row // 16); in every draw one owner gets exactly 3 from every index. Likewise with owner = tile_col // 8: at most 3 from one index of tile to one owner, and one owner gets exactly 3 from every index.
All inputs are finite; a program needn't handle non-finite values.
Results may differ from a plain program's by a relative error of at most 0.0052.
Values may be sent and summed in bfloat16 or wider, within the bound.
A program may use at most 64 MiB of HBM per device.

v0:
```python
import jax
import jax.numpy as jnp
from jax import lax
from jax.sharding import PartitionSpec as P

MEMBERS = 256
FLUX_DEV = 8
SOUND_DEV = 16


def sent_to_all(value, axis):
    size = lax.axis_size(axis)
    return lax.all_to_all(
        jnp.broadcast_to(value[None], (size, *value.shape)), axis, 0, 0, tiled=True
    )


def over_copies(value, axis):
    return sent_to_all(value, axis).sum(axis=0)


def slot_of(owners, capacity):
    entries = owners.shape[0]
    position = jnp.arange(entries)
    earlier = (owners[:, None] == owners[None, :]) & (position[None, :] < position[:, None])
    return owners * capacity + jnp.sum(earlier.astype(jnp.int32), axis=1)


def invert(slot_ids, slot_total):
    matches = slot_ids[None, :] == jnp.arange(slot_total)[:, None]
    sources = jnp.sum(jnp.where(matches, jnp.arange(slot_ids.shape[0])[None, :], 0), axis=1)
    return (sources, jnp.any(matches, axis=1))


def to_slots(values, sources, usage_flags):
    placed = jnp.take(values, sources, axis=1)
    return jnp.where(usage_flags[None, :, None], placed, jnp.zeros_like(placed))


def body(footprints, tile_row, tile_col, prior_flux, observed, precision_weight):
    devices_tile = lax.axis_size("tile")
    tile_count = footprints.shape[0]
    tile_size = footprints.shape[1]
    capacity = tile_count // devices_tile + max(1, tile_count // (2 * devices_tile))
    slot_total = devices_tile * capacity
    local_members = prior_flux.shape[0]
    local_sum = jnp.sum(prior_flux.astype(jnp.float32), axis=0)
    ensemble_sum = over_copies(local_sum, "mem")
    ensemble_mean = ensemble_sum / MEMBERS
    member_deviations = (prior_flux.astype(jnp.float32) - ensemble_mean[None, :]).astype(
        jnp.bfloat16
    )
    row_owner = tile_row // SOUND_DEV
    row_local = tile_row % SOUND_DEV
    col_owner = tile_col // FLUX_DEV
    col_local = tile_col % FLUX_DEV
    row_slot = slot_of(row_owner, capacity)
    col_slot = slot_of(col_owner, capacity)
    row_source, row_used = invert(row_slot, slot_total)
    col_source, col_used = invert(col_slot, slot_total)
    gathered = lax.all_gather(member_deviations, "tile", axis=1, tiled=True)
    retrieved_blocks = jnp.take(gathered.reshape(local_members, -1, tile_size), tile_col, axis=1)
    forward_terms = jnp.einsum(
        "mtk,trk->mtr", retrieved_blocks, footprints, preferred_element_type=jnp.float32
    )
    row_index = jnp.where(row_used, jnp.take(row_local, row_source), SOUND_DEV)
    sent_terms = to_slots(forward_terms, row_source, row_used)
    got_terms, got_rows = (
        lax.all_to_all(
            sent_terms.astype(jnp.bfloat16), "tile", split_axis=1, concat_axis=1, tiled=True
        ).astype(sent_terms.dtype),
        lax.all_to_all(row_index[None, :], "tile", split_axis=1, concat_axis=1, tiled=True),
    )
    got_rows = got_rows[0]
    row_match = (got_rows[None, :] == jnp.arange(SOUND_DEV)[:, None]).astype(jnp.float32)
    modelled = jnp.einsum("ds,msk->mdk", row_match, got_terms, precision=lax.Precision.HIGHEST)
    targets = observed.reshape(local_members, SOUND_DEV, tile_size)
    obs_weight = (precision_weight.astype(jnp.float32) / 8.0).reshape(SOUND_DEV, tile_size)
    weighted = (obs_weight[None, :, :] * (modelled - targets)).astype(jnp.bfloat16)
    reply_rows = jnp.take(weighted, jnp.minimum(got_rows, SOUND_DEV - 1), axis=1)
    returned = lax.all_to_all(reply_rows, "tile", split_axis=1, concat_axis=1, tiled=True)
    residual_tiles = jnp.take(returned, row_slot, axis=1)
    backward_terms = jnp.einsum(
        "mtr,trk->mtk", residual_tiles, footprints, preferred_element_type=jnp.float32
    )
    col_index = jnp.where(col_used, jnp.take(col_local, col_source), FLUX_DEV)
    sent_back = to_slots(backward_terms, col_source, col_used)
    got_back, got_cols = (
        lax.all_to_all(
            sent_back.astype(jnp.bfloat16), "tile", split_axis=1, concat_axis=1, tiled=True
        ).astype(sent_back.dtype),
        lax.all_to_all(col_index[None, :], "tile", split_axis=1, concat_axis=1, tiled=True),
    )
    col_match = (got_cols[0][None, :] == jnp.arange(FLUX_DEV)[:, None]).astype(jnp.float32)
    reduced_total = jnp.einsum("fs,msk->mfk", col_match, got_back, precision=lax.Precision.HIGHEST)
    gradient = reduced_total.reshape(local_members, FLUX_DEV * tile_size)
    return gradient


def solution(mesh):
    in_specs = (
        P("tile", None, None),
        P("tile"),
        P("tile"),
        P("mem", "tile"),
        P("mem", "tile"),
        P("tile"),
    )
    out_specs = P("mem", "tile")
    return jax.shard_map(body, mesh=mesh, in_specs=in_specs, out_specs=out_specs, check_vma=False)
```

profile of v0, /device:TPU:2, one launch (start us, length us, event | category | flops | bytes accessed | tf_op | source)
XLA Modules:
  0.0 407.8 jit_solution(12967651325447050244)
XLA Ops:
  6.5 0.9 convert_reduce_fusion
  7.5 9.6 %all_to_all.39 = f32[4,1,1024]{2,1,0:T(1,128)S(1)} all-to-all(f32[4,1,1024]{2,1,0:T(1,128)S(1)} %broadcast_in_dim.122), channel_id=1, replica_groups=mesh['tile'=64,'mem'=4] {'mem'}, dimensions={0} | all-to-all | bytes 32768 | tf_op jit(solution)/shard_map/all_to_all | solution.py:13
  17.2 1.6 fusion.26
  19.8 1.6 gather_fusion.3
  21.5 0.7 all_to_all.25
  22.2 12.0 %all-to-all-start = ((s32[1,64,3]{2,0,1:T(1,128)}), s32[1,64,3]{2,0,1:T(1,128)S(1)}, u32[]{:S(2)}, u32[]{:S(2)}) async-start(s32[1,64,3]{2,0,1:T(1,128)} %bitcast), calls=%async_computation | async-start | bytes 65536 | tf_op jit(solution)/shard_map/all_to_all | solution.py:72
  35.6 66.0 %all-gather.2.cloned.1.call-done = bf16[64,65536]{1,0:T(8,128)(2,1)} async-done(((bf16[64,1024]{1,0:T(8,128)(2,1)}), bf16[64,65536]{1,0:T(8,128)(2,1)}) %all-gather.2.cloned.1.call-update) | async-done | bytes 8388624 | tf_op jit(solution)/shard_map/all_gather | solution.py:61
  101.5 9.0 %copy_bitcast_fusion = bf16[64,512,128]{2,0,1:T(8,128)(2,1)} fusion(bf16[64,65536]{1,0:T(8,128)(2,1)} %all-gather.2.cloned.1.call-done), kind=kLoop, calls=%fused_computation.7 | loop fusion | bytes 16777216 | tf_op jit(solution)/shard_map/reshape | solution.py:62
  110.5 5.5 %gather_fusion = bf16[128,64,128]{2,1,0:T(8,128)(2,1)} fusion(bf16[64,512,128]{2,0,1:T(8,128)(2,1)} %copy_bitcast_fusion, s32[1024]{0:T(1024)S(1)} %pad_clamp_fusion.3), kind=kCustom, calls=%fused_computation.4 | custom fusion | bytes 4194816 | tf_op jit(solution)/shard_map/jit(_take)/gather | solution.py:62
  116.1 5.8 %convolution_bitcast_fusion.1 = bf16[64,128,128]{2,0,1:T(8,128)(2,1)S(1)} fusion(bf16[128,128,128]{2,1,0:T(8,128)(2,1)} %param.10, bf16[128,64,128]{2,1,0:T(8,128)(2,1)} %gather_fusion, pred[128]{0:T(512)(128)(4,1)S(1)} %compare_and_fusion.2), kind=kOutput, calls=%fused_computation.18 | convolution fusion | flops 269484032 | bytes 8388736 | tf_op jit(solution)/shard_map/mtk,trk->mtr/dot_general | solution.py:63
  121.8 2.7 gather_fusion.4
  124.6 4.3 %fusion.1 = bf16[64,192,128]{2,0,1:T(8,128)(2,1)} fusion(bf16[192,64,128]{2,1,0:T(8,128)(2,1)} %gather_fusion.4, pred[192]{0:T(512)(128)(4,1)S(1)} %get-tuple-element.14, pred[192]{0:T(512)(128)(4,1)S(1)} %fusion.27), kind=kLoop, calls=%fused_computation.11 | loop fusion | flops 3145728 | bytes 6291840 | tf_op jit(solution)/shard_map/convert_element_type | solution.py:70
  128.8 7.8 %all-to-all-start.2 = ((bf16[64,192,128]{2,0,1:T(8,128)(2,1)}), bf16[64,192,128]{2,0,1:T(8,128)(2,1)S(1)}, u32[]{:S(2)}, u32[]{:S(2)}) async-start(bf16[64,192,128]{2,0,1:T(8,128)(2,1)} %fusion.1), calls=%async_computation.2 | async-start | bytes 6291456 | tf_op jit(solution)/shard_map/all_to_all | solution.py:69
  136.7 1.9 copy.34
  139.1 0.7 minimum_reduce_fusion
  140.2 70.2 %all-to-all-done.2 = bf16[64,192,128]{2,0,1:T(8,128)(2,1)S(1)} async-done(((bf16[64,192,128]{2,0,1:T(8,128)(2,1)}), bf16[64,192,128]{2,0,1:T(8,128)(2,1)S(1)}, u32[]{:S(2)}, u32[]{:S(2)}) %all-to-all-start.2) | async-done | bytes 3145760 | tf_op jit(solution)/shard_map/all_to_all | solution.py:69
  210.4 2.8 fusion.21
  213.3 1.2 gather_fusion.1
  214.5 2.1 select_bitcast_fusion
  216.6 5.4 %all-to-all-start.3 = ((bf16[64,192,128]{2,0,1:T(8,128)(2,1)}), bf16[64,192,128]{2,0,1:T(8,128)(2,1)S(1)}, u32[]{:S(2)}, u32[]{:S(2)}) async-start(bf16[64,192,128]{2,0,1:T(8,128)(2,1)} %select_bitcast_fusion), calls=%async_computation.3 | async-start | bytes 6291456 | tf_op jit(solution)/shard_map/all_to_all | solution.py:81
  222.3 1.6 gather_fusion.6
  224.0 0.8 all_to_all.31
  224.8 70.9 %all-to-all-done.3 = bf16[64,192,128]{2,0,1:T(8,128)(2,1)S(1)} async-done(((bf16[64,192,128]{2,0,1:T(8,128)(2,1)}), bf16[64,192,128]{2,0,1:T(8,128)(2,1)S(1)}, u32[]{:S(2)}, u32[]{:S(2)}) %all-to-all-start.3) | async-done | bytes 3145760 | tf_op jit(solution)/shard_map/all_to_all | solution.py:81
  295.8 5.4 %all-to-all-start.5 = ((s32[1,64,3]{2,0,1:T(1,128)}), s32[1,64,3]{2,0,1:T(1,128)S(1)}, u32[]{:S(2)}, u32[]{:S(2)}) async-start(s32[1,64,3]{2,0,1:T(1,128)} %bitcast.12), calls=%async_computation.5 | async-start | bytes 65536 | tf_op jit(solution)/shard_map/all_to_all | solution.py:92
  301.2 2.2 gather_fusion.2
  303.4 4.1 %convolution_bitcast_fusion = bf16[64,128,128]{2,0,1:T(8,128)(2,1)S(1)} fusion(bf16[128,128,128]{2,1,0:T(8,128)(2,1)} %param.10, bf16[128,64,128]{2,1,0:T(8,128)(2,1)} %gather_fusion.2, pred[128]{0:T(512)(128)(4,1)S(1)} %get-tuple-element.11), kind=kOutput, calls=%fused_computation.17 | convolution fusion | flops 269484032 | bytes 8388736 | tf_op jit(solution)/shard_map/mtr,trk->mtk/dot_general | solution.py:83
  307.5 2.7 gather_fusion.5
  310.2 4.3 %fusion = bf16[64,192,128]{2,0,1:T(8,128)(2,1)} fusion(bf16[192,64,128]{2,1,0:T(8,128)(2,1)} %gather_fusion.5, pred[192]{0:T(512)(128)(4,1)S(1)} %get-tuple-element.10, pred[192]{0:T(512)(128)(4,1)S(1)} %fusion.28), kind=kLoop, calls=%fused_computation.9 | loop fusion | flops 3145728 | bytes 6291840 | tf_op jit(solution)/shard_map/convert_element_type | solution.py:90
  314.5 10.3 %all-to-all-start.4 = ((bf16[64,192,128]{2,0,1:T(8,128)(2,1)}), bf16[64,192,128]{2,0,1:T(8,128)(2,1)S(1)}, u32[]{:S(2)}, u32[]{:S(2)}) async-start(bf16[64,192,128]{2,0,1:T(8,128)(2,1)} %fusion), calls=%async_computation.4 | async-start | bytes 6291456 | tf_op jit(solution)/shard_map/all_to_all | solution.py:89
  325.5 73.0 %all-to-all-done.4 = bf16[64,192,128]{2,0,1:T(8,128)(2,1)S(1)} async-done(((bf16[64,192,128]{2,0,1:T(8,128)(2,1)}), bf16[64,192,128]{2,0,1:T(8,128)(2,1)S(1)}, u32[]{:S(2)}, u32[]{:S(2)}) %all-to-all-start.4) | async-done | bytes 3145760 | tf_op jit(solution)/shard_map/all_to_all | solution.py:89
  398.5 1.7 fusion.2
  400.2 0.8 copy.50
  (39 shorter events, 4.6 us)
Async XLA Ops:
  6.5 95.0 %all-gather.2.cloned.1.call-start = ((), (), s32[]{:S(2)}) async-start(), calls=%async_computation.6 | async-start | bytes 8519680 | tf_op jit(solution)/shard_map/all_gather | solution.py:61
  22.2 106.6 %all-to-all-start = ((s32[1,64,3]{2,0,1:T(1,128)}), s32[1,64,3]{2,0,1:T(1,128)S(1)}, u32[]{:S(2)}, u32[]{:S(2)}) async-start(s32[1,64,3]{2,0,1:T(1,128)} %bitcast), calls=%async_computation | async-start | bytes 65536 | tf_op jit(solution)/shard_map/all_to_all | solution.py:72
  128.8 9.8 %copy-start = (s32[2048]{0:T(1024)S(1)}, s32[2048]{0:T(1024)}, u32[]{:S(2)}) copy-start(s32[2048]{0:T(1024)} %param.15) | copy-start | bytes 24580
  128.8 81.6 %all-to-all-start.2 = ((bf16[64,192,128]{2,0,1:T(8,128)(2,1)}), bf16[64,192,128]{2,0,1:T(8,128)(2,1)S(1)}, u32[]{:S(2)}, u32[]{:S(2)}) async-start(bf16[64,192,128]{2,0,1:T(8,128)(2,1)} %fusion.1), calls=%async_computation.2 | async-start | bytes 6291456 | tf_op jit(solution)/shard_map/all_to_all | solution.py:69
  216.6 79.2 %all-to-all-start.3 = ((bf16[64,192,128]{2,0,1:T(8,128)(2,1)}), bf16[64,192,128]{2,0,1:T(8,128)(2,1)S(1)}, u32[]{:S(2)}, u32[]{:S(2)}) async-start(bf16[64,192,128]{2,0,1:T(8,128)(2,1)} %select_bitcast_fusion), calls=%async_computation.3 | async-start | bytes 6291456 | tf_op jit(solution)/shard_map/all_to_all | solution.py:81
  295.8 18.7 %all-to-all-start.5 = ((s32[1,64,3]{2,0,1:T(1,128)}), s32[1,64,3]{2,0,1:T(1,128)S(1)}, u32[]{:S(2)}, u32[]{:S(2)}) async-start(s32[1,64,3]{2,0,1:T(1,128)} %bitcast.12), calls=%async_computation.5 | async-start | bytes 65536 | tf_op jit(solution)/shard_map/all_to_all | solution.py:92
  314.5 84.0 %all-to-all-start.4 = ((bf16[64,192,128]{2,0,1:T(8,128)(2,1)}), bf16[64,192,128]{2,0,1:T(8,128)(2,1)S(1)}, u32[]{:S(2)}, u32[]{:S(2)}) async-start(bf16[64,192,128]{2,0,1:T(8,128)(2,1)} %fusion), calls=%async_computation.4 | async-start | bytes 6291456 | tf_op jit(solution)/shard_map/all_to_all | solution.py:89
Sparse Core Ops, SparseCore 0:
  18.9 82.6 all-gather.1
where the time goes:
time: 409 us; the launch traced here: 408 us
  waiting for transfers between devices  280 us (68%)
  starting transfers between devices  41 us (10%)
  local copies, waits for them, and re-layouts  31.6 us (8%)
  other arithmetic  17.4 us (4%)
  matrix products  14.4 us (4%)
  between operations  13.6 us (3%)
  blocking collectives  9.63 us (2%)
    all_to_all x1, waiting for transfers between devices, body(): lax.all_to_all(sent_back.astype(jnp.bfloat16), 'tile', split_axis=1, conc...  73 us
    all_to_all x1, waiting for transfers between devices, body(): lax.all_to_all(reply_rows, 'tile', split_axis=1, concat_axis=1, tiled=True)  70.9 us
    all_to_all x1, waiting for transfers between devices, body(): lax.all_to_all(sent_terms.astype(jnp.bfloat16), 'tile', split_axis=1, con...  70.2 us
    all_gather x1, waiting for transfers between devices, body(): gathered = lax.all_gather(member_deviations, 'tile', axis=1, tiled=True)  66 us
    all_to_all x1, starting transfers between devices, body(): lax.all_to_all(row_index[None, :], 'tile', split_axis=1, concat_axis=1, t...  12 us
    all_to_all x1, starting transfers between devices, body(): lax.all_to_all(sent_back.astype(jnp.bfloat16), 'tile', split_axis=1, conc...  10.3 us
    all_to_all x1, blocking collectives, sent_to_all(): lax.all_to_all(jnp.broadcast_to(value[None], (size, *value.shape)), axis,...  9.63 us
    reshape x1, local copies, waits for them, and re-layouts, body(): gathered.reshape(local_members, -1, tile_size)  9.01 us
  transfers between devices with their start and end apart: 6, of which 4 were waited for; matrix products, arithmetic and copies ran while one was open for 12% of the time, Pallas kernels for 0%

commit v1 on v0

--- a/solution.py
+++ b/solution.py
@@ -58,7 +58,9 @@
     col_slot = slot_of(col_owner, capacity)
     row_source, row_used = invert(row_slot, slot_total)
     col_source, col_used = invert(col_slot, slot_total)
-    gathered = lax.all_gather(member_deviations, "tile", axis=1, tiled=True)
+    gathered = jnp.concatenate(
+        lax.all_to_all(jnp.stack([member_deviations] * lax.axis_size("tile")), "tile", 0, 0), axis=1
+    )
     retrieved_blocks = jnp.take(gathered.reshape(local_members, -1, tile_size), tile_col, axis=1)
     forward_terms = jnp.einsum(
         "mtk,trk->mtr", retrieved_blocks, footprints, preferred_element_type=jnp.float32

time: 409 us -> 551 us (1.35)
  waiting for transfers between devices: 280 us -> 396 us
  local copies, waits for them, and re-layouts: 31.6 us -> 63.5 us
  between operations: 13.6 us -> 0.27 us
  starting transfers between devices: 41 us -> 51.3 us
    all_to_all x0 -> x1, waiting for transfers between devices: none -> 182 us  [body(): lax.all_to_all(jnp.stack([member_deviations] * lax.axis_size('tile')), 't...]
    all_gather x1 -> x0, waiting for transfers between devices: 66 us -> none  [body(): gathered = lax.all_gather(member_deviations, 'tile', axis=1, tiled=True)]
    another operation x0 -> x3, local copies, waits for them, and re-layouts: none -> 29.6 us  [the longest x2 25.3 us: body(): gathered.reshape(local_members, -1, tile_size)]
    all_to_all x0 -> x1, starting transfers between devices: none -> 12.3 us  [body(): lax.all_to_all(jnp.stack([member_deviations] * lax.axis_size('tile')), 't...]
  transfers between devices with their start and end apart: 6 -> 6, of which waited for: 4 -> 4; matrix products, arithmetic and copies ran while one was open for 12% -> 14% of each run, Pallas kernels for 0% -> 0%
where the time goes in v1:
time: 551 us; the launch traced here: 550 us
  waiting for transfers between devices  396 us (72%)
  local copies, waits for them, and re-layouts  63.5 us (12%)
  starting transfers between devices  51.3 us (9%)
  other arithmetic  14.8 us (3%)
  matrix products  14.4 us (3%)
  blocking collectives  9.63 us (2%)
    all_to_all x1, waiting for transfers between devices, body(): lax.all_to_all(jnp.stack([member_deviations] * lax.axis_size('tile')), 't...  182 us
    all_to_all x1, waiting for transfers between devices, body(): lax.all_to_all(sent_back.astype(jnp.bfloat16), 'tile', split_axis=1, conc...  73 us
    all_to_all x1, waiting for transfers between devices, body(): lax.all_to_all(reply_rows, 'tile', split_axis=1, concat_axis=1, tiled=True)  70.9 us
    all_to_all x1, waiting for transfers between devices, body(): lax.all_to_all(sent_terms.astype(jnp.bfloat16), 'tile', split_axis=1, con...  70.2 us
    another operation x2, local copies, waits for them, and re-layouts, body(): gathered.reshape(local_members, -1, tile_size)  25.3 us
    all_to_all x1, starting transfers between devices, body(): lax.all_to_all(jnp.stack([member_deviations] * lax.axis_size('tile')), 't...  12.3 us
    reshape x1, local copies, waits for them, and re-layouts, body(): jnp.concatenate(lax.all_to_all(jnp.stack([member_deviations] * lax.axis_s...  11.3 us
  transfers between devices with their start and end apart: 6, of which 4 were waited for; matrix products, arithmetic and copies ran while one was open for 14% of the time, Pallas kernels for 0%

profile of v1, /device:TPU:2, one launch (start us, length us, event | category | flops | bytes accessed | tf_op | source)
XLA Modules:
  0.0 550.3 jit_solution(1539384801928295491)
XLA Ops:
  0.0 0.9 convert_reduce_fusion
  1.0 9.6 %all_to_all.44 = f32[4,1,1024]{2,1,0:T(1,128)S(1)} all-to-all(f32[4,1,1024]{2,1,0:T(1,128)S(1)} %broadcast_in_dim.122), channel_id=1, replica_groups=mesh['tile'=64,'mem'=4] {'mem'}, dimensions={0} | all-to-all | bytes 32768 | tf_op jit(solution)/shard_map/all_to_all | solution.py:13
  10.6 0.9 fusion.26
  11.6 4.3 stack.2
  15.8 12.3 %all-to-all-start.2 = ((bf16[64,64,1024]{2,1,0:T(8,128)(2,1)}), bf16[64,64,1024]{2,1,0:T(8,128)(2,1)}, u32[]{:S(2)}, u32[]{:S(2)}) async-start(bf16[64,64,1024]{2,1,0:T(8,128)(2,1)} %stack.2), calls=%async_computation.2 | async-start | bytes 16777216 | tf_op jit(solution)/shard_map/all_to_all | solution.py:62
  28.5 1.6 gather_fusion.3
  31.0 182.2 %all-to-all-done.2 = bf16[64,64,1024]{2,1,0:T(8,128)(2,1)} async-done(((bf16[64,64,1024]{2,1,0:T(8,128)(2,1)}), bf16[64,64,1024]{2,1,0:T(8,128)(2,1)}, u32[]{:S(2)}, u32[]{:S(2)}) %all-to-all-start.2) | async-done | bytes 8388640 | tf_op jit(solution)/shard_map/all_to_all | solution.py:62
  213.2 7.4 %all-to-all-start = ((s32[1,64,3]{2,0,1:T(1,128)}), s32[1,64,3]{2,0,1:T(1,128)S(1)}, u32[]{:S(2)}, u32[]{:S(2)}) async-start(s32[1,64,3]{2,0,1:T(1,128)} %bitcast), calls=%async_computation | async-start | bytes 65536 | tf_op jit(solution)/shard_map/all_to_all | solution.py:74
  220.6 11.3 %copy.30 = bf16[64,64,1024]{2,1,0:T(8,128)(2,1)} copy(bf16[64,64,1024]{2,0,1:T(8,128)(2,1)} %bitcast.2) | data formatting | bytes 16777216 | tf_op jit(solution)/shard_map/reshape | solution.py:61
  231.9 13.3 %reshape_reshape.3 = bf16[64,512,128]{2,1,0:T(8,128)(2,1)} reshape(bf16[64,64,1024]{2,1,0:T(8,128)(2,1)} %copy.30) | data formatting | bytes 16777216 | tf_op jit(solution)/shard_map/reshape;reshape | solution.py:64
  245.2 12.0 %copy.31 = bf16[64,512,128]{2,0,1:T(8,128)(2,1)} copy(bf16[64,512,128]{2,1,0:T(8,128)(2,1)} %reshape_reshape.3) | data formatting | bytes 16777216 | tf_op jit(solution)/shard_map/reshape;reshape | solution.py:64
  257.2 5.5 %gather_fusion = bf16[128,64,128]{2,1,0:T(8,128)(2,1)} fusion(bf16[64,512,128]{2,0,1:T(8,128)(2,1)} %copy.31, s32[1024]{0:T(1024)S(1)} %pad_clamp_fusion.3), kind=kCustom, calls=%fused_computation.4 | custom fusion | bytes 4194816 | tf_op jit(solution)/shard_map/jit(_take)/gather | solution.py:64
  262.8 5.8 %convolution_bitcast_fusion.1 = bf16[64,128,128]{2,0,1:T(8,128)(2,1)S(1)} fusion(bf16[128,128,128]{2,1,0:T(8,128)(2,1)} %param.10, bf16[128,64,128]{2,1,0:T(8,128)(2,1)} %gather_fusion, pred[128]{0:T(512)(128)(4,1)S(1)} %compare_and_fusion.2), kind=kOutput, calls=%fused_computation.17 | convolution fusion | flops 269484032 | bytes 8388736 | tf_op jit(solution)/shard_map/mtk,trk->mtr/dot_general | solution.py:65
  268.5 2.7 gather_fusion.4
  271.2 4.3 fusion.1
  275.5 10.4 %all-to-all-start.3 = ((bf16[64,192,128]{2,0,1:T(8,128)(2,1)}), bf16[64,192,128]{2,0,1:T(8,128)(2,1)S(1)}, u32[]{:S(2)}, u32[]{:S(2)}) async-start(bf16[64,192,128]{2,0,1:T(8,128)(2,1)} %fusion.1), calls=%async_computation.3 | async-start | bytes 6291456 | tf_op jit(solution)/shard_map/all_to_all | solution.py:71
  286.0 1.9 copy.37
  289.5 70.2 %all-to-all-done.3 = bf16[64,192,128]{2,0,1:T(8,128)(2,1)S(1)} async-done(((bf16[64,192,128]{2,0,1:T(8,128)(2,1)}), bf16[64,192,128]{2,0,1:T(8,128)(2,1)S(1)}, u32[]{:S(2)}, u32[]{:S(2)}) %all-to-all-start.3) | async-done | bytes 3145760 | tf_op jit(solution)/shard_map/all_to_all | solution.py:71
  359.7 2.8 fusion.21
  362.6 1.2 gather_fusion.1
  363.8 2.1 select_bitcast_fusion
  365.8 5.4 all-to-all-start.4
  371.6 1.6 gather_fusion.6
  374.1 70.9 %all-to-all-done.4 = bf16[64,192,128]{2,0,1:T(8,128)(2,1)S(1)} async-done(((bf16[64,192,128]{2,0,1:T(8,128)(2,1)}), bf16[64,192,128]{2,0,1:T(8,128)(2,1)S(1)}, u32[]{:S(2)}, u32[]{:S(2)}) %all-to-all-start.4) | async-done | bytes 3145760 | tf_op jit(solution)/shard_map/all_to_all | solution.py:83
  445.0 5.4 all-to-all-start.6
  450.5 2.2 gather_fusion.2
  452.6 4.1 convolution_bitcast_fusion
  456.7 2.7 gather_fusion.5
  459.5 4.3 fusion
  463.7 10.3 %all-to-all-start.5 = ((bf16[64,192,128]{2,0,1:T(8,128)(2,1)}), bf16[64,192,128]{2,0,1:T(8,128)(2,1)S(1)}, u32[]{:S(2)}, u32[]{:S(2)}) async-start(bf16[64,192,128]{2,0,1:T(8,128)(2,1)} %fusion), calls=%async_computation.5 | async-start | bytes 6291456 | tf_op jit(solution)/shard_map/all_to_all | solution.py:91
  474.8 73.0 %all-to-all-done.5 = bf16[64,192,128]{2,0,1:T(8,128)(2,1)S(1)} async-done(((bf16[64,192,128]{2,0,1:T(8,128)(2,1)}), bf16[64,192,128]{2,0,1:T(8,128)(2,1)S(1)}, u32[]{:S(2)}, u32[]{:S(2)}) %all-to-all-start.5) | async-done | bytes 3145760 | tf_op jit(solution)/shard_map/all_to_all | solution.py:91
  547.8 1.7 fusion.2
  (45 shorter events, 5.6 us)
Async XLA Ops:
  15.8 12.4 %copy-start.2 = (s32[128]{0:T(128)S(1)}, s32[128]{0:T(128)}, u32[]{:S(2)}) copy-start(s32[128]{0:T(128)} %param.11) | copy-start | bytes 1540
  15.8 15.2 %copy-start.1 = (s32[128]{0:T(128)S(1)}, s32[128]{0:T(128)}, u32[]{:S(2)}) copy-start(s32[128]{0:T(128)} %param.12) | copy-start | bytes 1540
  15.8 197.4 %all-to-all-start.2 = ((bf16[64,64,1024]{2,1,0:T(8,128)(2,1)}), bf16[64,64,1024]{2,1,0:T(8,128)(2,1)}, u32[]{:S(2)}, u32[]{:S(2)}) async-start(bf16[64,64,1024]{2,1,0:T(8,128)(2,1)} %stack.2), calls=%async_computation.2 | async-start | bytes 16777216 | tf_op jit(solution)/shard_map/all_to_all | solution.py:62
  213.2 62.3 %all-to-all-start = ((s32[1,64,3]{2,0,1:T(1,128)}), s32[1,64,3]{2,0,1:T(1,128)S(1)}, u32[]{:S(2)}, u32[]{:S(2)}) async-start(s32[1,64,3]{2,0,1:T(1,128)} %bitcast), calls=%async_computation | async-start | bytes 65536 | tf_op jit(solution)/shard_map/all_to_all | solution.py:74
  275.5 12.4 %copy-start = (s32[2048]{0:T(1024)S(1)}, s32[2048]{0:T(1024)}, u32[]{:S(2)}) copy-start(s32[2048]{0:T(1024)} %param.15) | copy-start | bytes 24580
  275.5 84.2 %all-to-all-start.3 = ((bf16[64,192,128]{2,0,1:T(8,128)(2,1)}), bf16[64,192,128]{2,0,1:T(8,128)(2,1)S(1)}, u32[]{:S(2)}, u32[]{:S(2)}) async-start(bf16[64,192,128]{2,0,1:T(8,128)(2,1)} %fusion.1), calls=%async_computation.3 | async-start | bytes 6291456 | tf_op jit(solution)/shard_map/all_to_all | solution.py:71
  365.8 79.2 %all-to-all-start.4 = ((bf16[64,192,128]{2,0,1:T(8,128)(2,1)}), bf16[64,192,128]{2,0,1:T(8,128)(2,1)S(1)}, u32[]{:S(2)}, u32[]{:S(2)}) async-start(bf16[64,192,128]{2,0,1:T(8,128)(2,1)} %select_bitcast_fusion), calls=%async_computation.4 | async-start | bytes 6291456 | tf_op jit(solution)/shard_map/all_to_all | solution.py:83
  445.0 18.7 %all-to-all-start.6 = ((s32[1,64,3]{2,0,1:T(1,128)}), s32[1,64,3]{2,0,1:T(1,128)S(1)}, u32[]{:S(2)}, u32[]{:S(2)}) async-start(s32[1,64,3]{2,0,1:T(1,128)} %bitcast.13), calls=%async_computation.6 | async-start | bytes 65536 | tf_op jit(solution)/shard_map/all_to_all | solution.py:94
  463.7 84.0 %all-to-all-start.5 = ((bf16[64,192,128]{2,0,1:T(8,128)(2,1)}), bf16[64,192,128]{2,0,1:T(8,128)(2,1)S(1)}, u32[]{:S(2)}, u32[]{:S(2)}) async-start(bf16[64,192,128]{2,0,1:T(8,128)(2,1)} %fusion), calls=%async_computation.5 | async-start | bytes 6291456 | tf_op jit(solution)/shard_map/all_to_all | solution.py:91
